TPU v7x, 32 devices: a whole 2x2x4 slice. The times are simulated.
32 devices in a mesh: groups: 2 (over y), seq: 4 (over z), fsdp: 2 (over x), head: 2 (over core).
Axes of the slice: x: 2, y: 2, z: 4, core: 2. Of those that a mesh axis runs over, the one named last changes fastest.
Arguments:
- frames: bfloat16 [6144, 3072], P(('groups', 'seq')), parts along dimension 0, may hold values from -330 to 330
- modulation: float32 [4, 3072], P('groups'), parts along dimension 0, may hold values from -2.5 to 2.5
- w_qkv: bfloat16 [3072, 3, 2048], P('seq', None, ('fsdp', 'head')), may hold values from -0.109375 to 0.109375
- b_qkv: float32 [3, 2048], P(None, ('fsdp', 'head')), may hold values from -2.5 to 2.5
- qk_gain: float32 [2, 128], replicated, may hold values from 0.7 to 2.4
- block_lists: int32 [16, 27], P(('groups', 'seq')), parts along dimension 0, may hold values from -1 to 7, as said below
Outputs:
- attention: bfloat16 [6144, 2048], P(('groups', 'seq'), ('fsdp', 'head')), parts along dimension 0
There are 2 independent parts, one for each index of `groups`. A program takes and returns all parts, laid end to end along the dimension named above; an argument that names none is the same for every part. Nothing has to cross between parts.
Inputs may be any that keep to these rules, and one draw needn't show every extreme that they name: `block_lists`: tile g lies at width g // 2, time (g % 2) // 1 and height g % 1 of a 2 x 1 x 4 grid of tiles. Entry (a + 1) * 9 + (b + 1) * 3 + (c + 1) of row g, for a, b, c in -1, 0, 1, is the tile at time + a, height + b and width + c of tile g, or -1 where that tile is outside the grid or left out of the list. Entry 13 is always g.
All inputs are finite; a program needn't handle non-finite values.
Results may differ from a plain program's by a relative error of at most 0.0058.
Values may be sent and summed in bfloat16 or wider, within the bound.
No kernel may reach another device: no remote copies, remote signals or barrier semaphores. Data moves between devices by JAX's collectives and lax.ppermute only.
A program may use at most 128 MiB of HBM per device.

v0:
```python
import math
import jax
import jax.numpy as jnp
from jax import lax
from jax.sharding import PartitionSpec as P


def with_halo(shard, sides, width):
    for axis, dim in sides:
        devices, length = (lax.axis_size(axis), shard.shape[dim])
        up = [(i, (i + 1) % devices) for i in range(devices - 1)]
        down = [(j, i) for i, j in up]
        last = lax.slice_in_dim(shard, length - width, length, axis=dim)
        first = lax.slice_in_dim(shard, 0, width, axis=dim)
        before = lax.ppermute(last, axis, up)
        after = lax.ppermute(first, axis, down)
        shard = jnp.concatenate([before, shard, after], axis=dim)
    return shard


def normed_heads(tensor, gain_row, head_dim):
    shaped = tensor.reshape(tensor.shape[0], tensor.shape[1] // head_dim, head_dim)
    scaled = (
        shaped * lax.rsqrt(jnp.mean(shaped * shaped, axis=-1, keepdims=True) + 1e-06) * gain_row
    )
    return scaled.astype(jnp.bfloat16)


def reach_sides(key_rows, values):
    stacked = jnp.stack([key_rows, values], axis=0)
    return with_halo(stacked, (("seq", 1),), key_rows.shape[0])


def per_device(frames, modulation, w_qkv, b_qkv, qk_gain, block_lists):
    inputs = frames.astype(jnp.float32)
    average = jnp.mean(inputs, axis=-1, keepdims=True)
    centred = inputs - average
    variance = jnp.mean(centred * centred, axis=-1, keepdims=True)
    normed = centred * lax.rsqrt(variance + 1e-06) * (1.0 + modulation[0]) + modulation[1]
    normed = normed.astype(jnp.bfloat16)
    tokens = normed.shape[0]
    width_cols = w_qkv.shape[2]
    head_dim = qk_gain.shape[1]
    heads = width_cols // head_dim
    projected = jnp.einsum(
        "td,djc->tjc",
        normed,
        lax.all_gather(w_qkv, "seq", axis=0, tiled=True),
        preferred_element_type=jnp.float32,
    )
    projected = projected + b_qkv
    queries = normed_heads(projected[:, 0], qk_gain[0], head_dim)
    key_rows = normed_heads(projected[:, 1], qk_gain[1], head_dim)
    values = projected[:, 2].astype(jnp.bfloat16).reshape(tokens, heads, head_dim)
    neighbourhood = reach_sides(key_rows, values)
    position = lax.axis_index("seq")
    tile_dev = block_lists.shape[0]
    tile_len = tokens // tile_dev
    candidates = (position - 1) * tile_dev + jnp.arange(3 * tile_dev, dtype=jnp.int32)
    matches = (block_lists[:, :, None] == candidates[None, None, :]) & (
        block_lists[:, :, None] >= 0
    )
    allowed_tiles = jnp.any(matches, axis=1)
    allowed_keys = jnp.repeat(jnp.repeat(allowed_tiles, tile_len, axis=0), tile_len, axis=1)
    factor = 1.0 / math.sqrt(head_dim)
    scores = (
        jnp.einsum("qhd,khd->hqk", queries, neighbourhood[0], preferred_element_type=jnp.float32)
        * factor
    )
    weights = jnp.where(allowed_keys[None, :, :], jnp.exp(scores), 0.0)
    totals = jnp.sum(weights, axis=-1)
    mixture = jnp.einsum(
        "hqk,khd->qhd",
        weights.astype(jnp.bfloat16),
        neighbourhood[1],
        preferred_element_type=jnp.float32,
    )
    result = (mixture / jnp.transpose(totals)[:, :, None]).astype(jnp.bfloat16)
    return result.reshape(tokens, width_cols)


def solution(mesh):
    placed = (
        P(("groups", "seq"), None),
        P("groups", None),
        P("seq", None, ("fsdp", "head")),
        P(None, ("fsdp", "head")),
        P(),
        P(("groups", "seq"), None),
    )
    return jax.shard_map(
        per_device,
        mesh=mesh,
        in_specs=placed,
        out_specs=P(("groups", "seq"), ("fsdp", "head")),
        check_vma=False,
    )
```

profile of v0, /device:TPU:0, one launch (start us, length us, event | category | flops | bytes accessed | tf_op | source)
XLA Modules:
  0.0 278.2 jit_solution(9089081699902757114)
XLA Ops:
  6.5 4.3 %copy.27 = bf16[768,3,512]{0,2,1:T(8,128)(2,1)} copy(bf16[768,3,512]{2,0,1:T(8,128)(2,1)} %param.8) | data formatting | bytes 4718592 | tf_op args[2]
  10.9 3.2 %convert_reduce_fusion = f32[768]{0:T(1024)S(1)} fusion(bf16[768,3072]{1,0:T(8,128)(2,1)} %param.6), kind=kLoop, calls=%fused_computation.6 | loop fusion | flops 4717824 | bytes 4721664 | tf_op jit(solution)/shard_map/reduce_sum | solution.py:36
  14.1 0.5 copy-done
  14.6 1.4 fusion.7
  16.0 164.5 %all-gather.2.cloned.1.call-done = bf16[3072,3,512]{0,2,1:T(8,128)(2,1)} async-done(((bf16[768,3,512]{0,2,1:T(8,128)(2,1)}), bf16[3072,3,512]{0,2,1:T(8,128)(2,1)}) %all-gather.2.cloned.1.call-update) | async-done | bytes 9437200 | tf_op jit(solution)/shard_map/all_gather | solution.py:48
  180.5 11.9 %broadcast_add_fusion = f32[768,3,512]{0,2,1:T(8,128)S(1)} fusion(f32[3,512]{1,0:T(4,128)S(1)} %copy-done.8, bf16[3072,3,512]{0,2,1:T(8,128)(2,1)} %all-gather.2.cloned.1.call-done, bf16[768,3072]{1,0:T(8,128)(2,1)} %param.6, f32[3072]{0:T(1024)S(1)} %bitcast.43, f32[3072]{0:T(1024)S(1)} %bitcast.42, f32[768]{0:T(1024)S(1)} %add_rsqrt_fusion.2, ...), kind=kOutput, calls=%fused_computation.23 | convolution fusion | flops 7263092736 | bytes 18911232 | tf_op jit(solution)/shard_map/td,djc->tjc/dot_general | solution.py:45
  192.5 2.0 fusion.28
  194.5 0.4 copy.29
  194.9 1.5 reduce_sum.47
  196.4 3.0 %copy.28 = f32[1,768,4,128]{3,1,2,0:T(8,128)} copy(f32[1,768,4,128]{1,3,2,0:T(8,128)} %bitcast.37) | data formatting | bytes 3145728 | tf_op jit(solution)/shard_map/reshape;squeeze | solution.py:22
  199.5 1.9 multiply_convert_fusion.1
  201.4 1.3 pad_maximum_fusion.1
  202.6 1.3 collective-permute-start.1
  203.9 5.7 %collective-permute-start = (bf16[2,768,4,128]{3,1,2,0:T(8,128)(2,1)}, bf16[2,768,4,128]{3,1,2,0:T(8,128)(2,1)}, u32[]{:S(2)}, u32[]{:S(2)}) collective-permute-start(bf16[2,768,4,128]{3,1,2,0:T(8,128)(2,1)} %pad_maximum_fusion.1), channel_id=1, source_target_pairs={{0,4},{4,8},{8,12},{1,5},{5,9},{9,13},{2,6},{6,10},{10,14},{3,7},{... | collective-permute-start | bytes 4718600 | tf_op jit(solution)/shard_map/ppermute | solution.py:15
  209.7 0.2 and_reduce_fusion
  209.9 1.7 broadcast_in_dim.19
  211.6 5.4 %copy.30 = pred[768,2304]{1,0:T(8,128)(4,1)} copy(pred[768,2304]{0,1:T(8,128)(4,1)} %bitcast.36) | data formatting | bytes 3538944 | tf_op jit(solution)/shard_map/jit(_where)/broadcast_in_dim | solution.py:70
  217.0 1.6 copy.31
  218.8 22.4 %collective-permute-done.1 = bf16[2,768,4,128]{3,1,2,0:T(8,128)(2,1)} collective-permute-done((bf16[2,768,4,128]{3,1,2,0:T(8,128)(2,1)}, bf16[2,768,4,128]{3,1,2,0:T(8,128)(2,1)}, u32[]{:S(2)}, u32[]{:S(2)}) %collective-permute-start.1) | collective-permute-done | bytes 1572896 | tf_op jit(solution)/shard_map/ppermute | solution.py:16
  241.2 1.2 collective-permute-done
  242.4 2.0 pad_maximum_fusion
  244.4 12.9 %fusion = (f32[4,768]{1,0:T(4,128)S(1)}, f32[4,768,2304]{2,1,0:T(8,128)}) fusion(pred[768,2304]{1,0:T(8,128)(4,1)S(1)} %copy-done.2, bf16[2,2304,4,128]{3,1,2,0:T(8,128)(2,1)S(1)} %pad_maximum_fusion, f32[768,4,128]{2,0,1:T(8,128)S(1)} %copy-done.4, f32[128]{0:T(128)S(1)} %get-tuple-element.10, f32[768,4]{0,1:T(4,128)S(1)} %add_rsqrt_fusion), kind=kOutput, calls=%fused_computation.1 | convolution fusion | flops 1834349568 | bytes 34038272 | tf_op jit(solution)/shard_map/qhd,khd->hqk/dot_general | solution.py:67
  257.3 12.9 %fusion.21 = bf16[768,4,128]{0,2,1:T(8,128)(2,1)S(1)} fusion(f32[768,4]{0,1:T(4,128)S(1)} %bitcast.44, f32[4,768,2304]{2,1,0:T(8,128)} %get-tuple-element.13, pred[768,2304]{1,0:T(8,128)(4,1)S(1)} %copy-done.3, bf16[2,2304,4,128]{3,1,2,0:T(8,128)(2,1)} %copy-done.1), kind=kOutput, calls=%fused_computation.27 | convolution fusion | flops 1833959424 | bytes 33239040 | tf_op jit(solution)/shard_map/hqk,khd->qhd/dot_general | solution.py:72
  270.2 1.2 copy.33
  (30 shorter events, 0.4 us)
Async XLA Ops:
  6.5 4.3 %copy-start.6 = (f32[2,128]{1,0:T(2,128)S(1)}, f32[2,128]{1,0:T(2,128)}, u32[]{:S(2)}) copy-start(f32[2,128]{1,0:T(2,128)} %param.10) | copy-start | bytes 3076
  6.5 174.0 %all-gather.2.cloned.1.call-start = ((), (), s32[]{:S(2)}) async-start(), calls=%async_computation | async-start | bytes 11796480 | tf_op jit(solution)/shard_map/all_gather | solution.py:48
  10.9 3.8 %copy-start = (bf16[768,3072]{1,0:T(8,128)(2,1)S(1)}, bf16[768,3072]{1,0:T(8,128)(2,1)}, u32[]{:S(2)}) copy-start(bf16[768,3072]{1,0:T(8,128)(2,1)} %param.6) | copy-start | bytes 14155780
  10.9 5.1 %copy-start.5 = (f32[2,3072]{1,0:T(2,128)S(1)}, f32[2,3072]{1,0:T(2,128)}, u32[]{:S(2)}) copy-start(f32[2,3072]{1,0:T(2,128)} %param.7) | copy-start | bytes 73732
  10.9 169.6 %copy-start.8 = (f32[3,512]{1,0:T(4,128)S(1)}, f32[3,512]{1,0:T(4,128)}, u32[]{:S(2)}) copy-start(f32[3,512]{1,0:T(4,128)} %param.9) | copy-start | bytes 18436
  196.4 13.3 %copy-start.7 = (s32[2,27]{1,0:T(2,128)S(1)}, s32[2,27]{1,0:T(2,128)}, u32[]{:S(2)}) copy-start(s32[2,27]{1,0:T(2,128)} %param.11) | copy-start | bytes 652
  202.6 38.6 %collective-permute-start.1 = (bf16[2,768,4,128]{3,1,2,0:T(8,128)(2,1)}, bf16[2,768,4,128]{3,1,2,0:T(8,128)(2,1)}, u32[]{:S(2)}, u32[]{:S(2)}) collective-permute-start(bf16[2,768,4,128]{3,1,2,0:T(8,128)(2,1)} %pad_maximum_fusion.1), channel_id=1, source_target_pairs={{4,0},{8,4},{12,8},{5,1},{9,5},{13,9},{6,2},{10,6},{14,10},{7,3},{... | collective-permute-start | bytes 4718600 | tf_op jit(solution)/shard_map/ppermute | solution.py:16
  203.9 38.4 %collective-permute-start = (bf16[2,768,4,128]{3,1,2,0:T(8,128)(2,1)}, bf16[2,768,4,128]{3,1,2,0:T(8,128)(2,1)}, u32[]{:S(2)}, u32[]{:S(2)}) collective-permute-start(bf16[2,768,4,128]{3,1,2,0:T(8,128)(2,1)} %pad_maximum_fusion.1), channel_id=1, source_target_pairs={{0,4},{4,8},{8,12},{1,5},{5,9},{9,13},{2,6},{6,10},{10,14},{3,7},{... | collective-permute-start | bytes 4718600 | tf_op jit(solution)/shard_map/ppermute | solution.py:15
  218.8 25.6 %copy-start.2 = (pred[768,2304]{1,0:T(8,128)(4,1)S(1)}, pred[768,2304]{1,0:T(8,128)(4,1)}, u32[]{:S(2)}) copy-start(pred[768,2304]{1,0:T(8,128)(4,1)} %copy.30) | copy-start | bytes 5308420
  218.8 25.6 %copy-start.4 = (f32[768,4,128]{2,0,1:T(8,128)S(1)}, f32[768,4,128]{2,0,1:T(8,128)}, u32[]{:S(2)}) copy-start(f32[768,4,128]{2,0,1:T(8,128)} %copy.31) | copy-start | bytes 4718596
  244.4 12.9 %copy-start.1 = (bf16[2,2304,4,128]{3,1,2,0:T(8,128)(2,1)}, bf16[2,2304,4,128]{3,1,2,0:T(8,128)(2,1)S(1)}, u32[]{:S(2)}) copy-start(bf16[2,2304,4,128]{3,1,2,0:T(8,128)(2,1)S(1)} %pad_maximum_fusion) | copy-start | bytes 14155780
  244.4 12.9 %copy-start.3 = (pred[768,2304]{1,0:T(8,128)(4,1)S(1)}, pred[768,2304]{1,0:T(8,128)(4,1)}, u32[]{:S(2)}) copy-start(pred[768,2304]{1,0:T(8,128)(4,1)} %copy.30) | copy-start | bytes 5308420
Sparse Core Ops, SparseCore 0:
  11.0 169.4 all-gather.1
where the time goes:
time: 279 us; the launch traced here: 278 us
  waiting for transfers between devices  188 us (67%)
  matrix products  37.7 us (14%)
  local copies, waits for them, and re-layouts  18.3 us (7%)
  other arithmetic  13.7 us (5%)
  between operations  13.6 us (5%)
  starting transfers between devices  7 us (3%)
    all_gather x1, waiting for transfers between devices, per_device(): lax.all_gather(w_qkv, 'seq', axis=0, tiled=True)  164 us
    ppermute x1, waiting for transfers between devices, with_halo(): after = lax.ppermute(first, axis, down)  22.4 us
    dot_general x1, matrix products, per_device(): jnp.einsum('qhd,khd->hqk', queries, neighbourhood[0], preferred_element_t...  12.9 us
    dot_general x1, matrix products, per_device(): jnp.einsum('hqk,khd->qhd', weights.astype(jnp.bfloat16), neighbourhood[1]...  12.9 us
    dot_general x1, matrix products, per_device(): jnp.einsum('td,djc->tjc', normed, lax.all_gather(w_qkv, 'seq', axis=0, ti...  11.9 us
    ppermute x1, starting transfers between devices, with_halo(): before = lax.ppermute(last, axis, up)  5.72 us
  transfers between devices with their start and end apart: 3, of which 3 were waited for; matrix products, arithmetic and copies ran while one was open for 5% of the time, Pallas kernels for 0%

commit v1 on v0

--- a/solution.py
+++ b/solution.py
@@ -42,12 +42,19 @@
     width_cols = w_qkv.shape[2]
     head_dim = qk_gain.shape[1]
     heads = width_cols // head_dim
-    projected = jnp.einsum(
-        "td,djc->tjc",
-        normed,
-        lax.all_gather(w_qkv, "seq", axis=0, tiled=True),
-        preferred_element_type=jnp.float32,
-    )
+    size, mine, span = (lax.axis_size("seq"), lax.axis_index("seq"), w_qkv.shape[0])
+    upward = [(i_2, (i_2 + 1) % size) for i_2 in range(size)]
+    current, projected = (w_qkv, None)
+    for step in range(size):
+        coming = lax.ppermute(current, "seq", upward) if step < size - 1 else None
+        take_in = jnp.einsum(
+            "td,djc->tjc",
+            lax.dynamic_slice_in_dim(normed, (mine - step) % size * span, current.shape[0], axis=1),
+            current,
+            preferred_element_type=jnp.float32,
+        )
+        projected = take_in if projected is None else projected + take_in
+        current = coming
     projected = projected + b_qkv
     queries = normed_heads(projected[:, 0], qk_gain[0], head_dim)
     key_rows = normed_heads(projected[:, 1], qk_gain[1], head_dim)

time: 279 us -> 246 us (0.88)
  waiting for transfers between devices: 188 us -> 164 us
  between operations: 13.6 us -> 0.37 us
  other arithmetic: 13.7 us -> 19.7 us
  starting transfers between devices: 7 us -> 10.1 us
    all_gather x1 -> x0, waiting for transfers between devices: 164 us -> none  [per_device(): lax.all_gather(w_qkv, 'seq', axis=0, tiled=True)]
    ppermute x0 -> x3, waiting for transfers between devices: none -> 143 us  [per_device(): coming = lax.ppermute(current, 'seq', upward) if step < size - 1 else None]
    convert_element_type x0 -> x1, other arithmetic: none -> 5.13 us  [per_device(): normed = normed.astype(jnp.bfloat16)]
    ppermute x0 -> x3, starting transfers between devices: none -> 3.08 us  [per_device(): coming = lax.ppermute(current, 'seq', upward) if step < size - 1 else None]
    dot_general x1 -> x4, matrix products: 11.9 us -> 10.1 us  [per_device(): jnp.einsum('td,djc->tjc', lax.dynamic_slice_in_dim(normed, (mine - step)...]
  transfers between devices with their start and end apart: 3 -> 5, of which waited for: 3 -> 5; matrix products, arithmetic and copies ran while one was open for 5% -> 11% of each run, Pallas kernels for 0% -> 0%
where the time goes in v1:
time: 246 us
  waiting for transfers between devices  164 us (67%)
  matrix products  35.8 us (15%)
  other arithmetic  19.7 us (8%)
  local copies, waits for them, and re-layouts  16.3 us (7%)
  starting transfers between devices  10.1 us (4%)
    ppermute x3, waiting for transfers between devices, per_device(): coming = lax.ppermute(current, 'seq', upward) if step < size - 1 else None  143 us
    ppermute x1, waiting for transfers between devices, with_halo(): after = lax.ppermute(first, axis, down)  19.7 us
    dot_general x1, matrix products, per_device(): jnp.einsum('hqk,khd->qhd', weights.astype(jnp.bfloat16), neighbourhood[1]...  12.9 us
    dot_general x1, matrix products, per_device(): jnp.einsum('qhd,khd->hqk', queries, neighbourhood[0], preferred_element_t...  12.8 us
    dot_general x4, matrix products, per_device(): jnp.einsum('td,djc->tjc', lax.dynamic_slice_in_dim(normed, (mine - step)...  10.1 us
    ppermute x1, starting transfers between devices, with_halo(): before = lax.ppermute(last, axis, up)  5.74 us
    broadcast_in_dim x1, local copies, waits for them, and re-layouts, per_device(): weights = jnp.where(allowed_keys[None, :, :], jnp.exp(scores), 0.0)  5.38 us
    convert_element_type x1, other arithmetic, per_device(): normed = normed.astype(jnp.bfloat16)  5.13 us
  transfers between devices with their start and end apart: 5, of which 5 were waited for; matrix products, arithmetic and copies ran while one was open for 11% of the time, Pallas kernels for 0%

profile of v1, /device:TPU:0, one launch (start us, length us, event | category | flops | bytes accessed | tf_op | source)
XLA Modules:
  0.0 245.9 jit_solution(13595194201801755748)
XLA Ops:
  0.0 2.8 %copy.31 = bf16[768,3,512]{0,2,1:T(8,128)(2,1)S(1)} copy(bf16[768,3,512]{2,0,1:T(8,128)(2,1)} %param.8) | data formatting | bytes 4718592 | tf_op args[2]
  2.9 3.1 %collective-permute-start = (bf16[768,3,512]{0,2,1:T(8,128)(2,1)S(1)}, bf16[768,3,512]{0,2,1:T(8,128)(2,1)S(1)}, u32[]{:S(2)}, u32[]{:S(2)}) collective-permute-start(bf16[768,3,512]{0,2,1:T(8,128)(2,1)S(1)} %copy.31), channel_id=1, source_target_pairs={{0,4},{4,8},{8,12},{12,0},{1,5},{5,9},{9,13},{13,1},{2,6},{6,10},{... | collective-permute-start | bytes 7077896 | tf_op jit(solution)/shard_map/ppermute | solution.py:49
  6.0 53.3 %collective-permute-done = bf16[768,3,512]{0,2,1:T(8,128)(2,1)S(1)} collective-permute-done((bf16[768,3,512]{0,2,1:T(8,128)(2,1)S(1)}, bf16[768,3,512]{0,2,1:T(8,128)(2,1)S(1)}, u32[]{:S(2)}, u32[]{:S(2)}) %collective-permute-start) | collective-permute-done | bytes 2359328 | tf_op jit(solution)/shard_map/ppermute | solution.py:49
  59.2 3.9 %convert_reduce_fusion = f32[768]{0:T(1024)S(1)} fusion(bf16[768,3072]{1,0:T(8,128)(2,1)} %param.6), kind=kLoop, calls=%fused_computation.6 | loop fusion | flops 4717824 | bytes 4721664 | tf_op jit(solution)/shard_map/reduce_sum | solution.py:36
  64.5 49.0 %collective-permute-done.1 = bf16[768,3,512]{0,2,1:T(8,128)(2,1)} collective-permute-done((bf16[768,3,512]{0,2,1:T(8,128)(2,1)S(1)}, bf16[768,3,512]{0,2,1:T(8,128)(2,1)}, u32[]{:S(2)}, u32[]{:S(2)}) %collective-permute-start.1) | collective-permute-done | bytes 2359328 | tf_op jit(solution)/shard_map/ppermute | solution.py:49
  113.7 5.1 %fusion.10 = bf16[768,3072]{1,0:T(8,128)(2,1)S(1)} fusion(bf16[768,3072]{1,0:T(8,128)(2,1)} %param.6, f32[3072]{0:T(1024)S(1)} %bitcast.52, f32[3072]{0:T(1024)S(1)} %bitcast.51, f32[768]{0:T(1024)S(1)} %add_rsqrt_fusion.2, f32[768]{0:T(1024)S(1)} %broadcast_multiply_fusion), kind=kLoop, calls=%fused_computation.12 | loop fusion | flops 14155776 | bytes 9467904 | tf_op jit(solution)/shard_map/convert_element_type | solution.py:40
  118.8 2.0 fusion.18
  120.9 2.1 fusion.16
  123.0 3.7 %fusion.14 = f32[768,3,512]{0,2,1:T(8,128)S(1)} fusion(bf16[768,3,512]{0,2,1:T(8,128)(2,1)} %collective-permute-done.1, bf16[768,3072]{1,0:T(8,128)(2,1)S(1)} %fusion.10, s32[]{:T(128)S(6)} %select_n.40), kind=kOutput, calls=%fused_computation.26 | convolution fusion | flops 1811939328 | bytes 8257540 | tf_op jit(solution)/shard_map/td,djc->tjc/dot_general | solution.py:50
  126.7 40.4 %collective-permute-done.2 = bf16[768,3,512]{0,2,1:T(8,128)(2,1)S(1)} collective-permute-done((bf16[768,3,512]{0,2,1:T(8,128)(2,1)}, bf16[768,3,512]{0,2,1:T(8,128)(2,1)S(1)}, u32[]{:S(2)}, u32[]{:S(2)}) %collective-permute-start.2) | collective-permute-done | bytes 2359328 | tf_op jit(solution)/shard_map/ppermute | solution.py:49
  167.1 2.3 add_add_fusion
  169.5 2.0 fusion.34
  171.9 1.5 reduce_sum.47
  173.4 3.0 %copy.32 = f32[1,768,4,128]{3,1,2,0:T(8,128)} copy(f32[1,768,4,128]{1,3,2,0:T(8,128)} %bitcast.47) | data formatting | bytes 3145728 | tf_op jit(solution)/shard_map/reshape;squeeze | solution.py:22
  176.5 1.9 multiply_convert_fusion.1
  178.3 1.5 pad_maximum_fusion.1
  181.1 5.7 %collective-permute-start.3 = (bf16[2,768,4,128]{3,1,2,0:T(8,128)(2,1)}, bf16[2,768,4,128]{3,1,2,0:T(8,128)(2,1)}, u32[]{:S(2)}, u32[]{:S(2)}) collective-permute-start(bf16[2,768,4,128]{3,1,2,0:T(8,128)(2,1)} %pad_maximum_fusion.1), channel_id=1, source_target_pairs={{0,4},{4,8},{8,12},{1,5},{5,9},{9,13},{2,6},{6,10},{10,14},{3,7},{... | collective-permute-start | bytes 4718600 | tf_op jit(solution)/shard_map/ppermute | solution.py:15
  187.1 1.7 broadcast_in_dim.19
  188.8 5.4 %copy.34 = pred[768,2304]{1,0:T(8,128)(4,1)} copy(pred[768,2304]{0,1:T(8,128)(4,1)} %bitcast.46) | data formatting | bytes 3538944 | tf_op jit(solution)/shard_map/jit(_where)/broadcast_in_dim | solution.py:77
  194.2 1.6 copy.35
  196.0 19.7 %collective-permute-done.4 = bf16[2,768,4,128]{3,1,2,0:T(8,128)(2,1)} collective-permute-done((bf16[2,768,4,128]{3,1,2,0:T(8,128)(2,1)}, bf16[2,768,4,128]{3,1,2,0:T(8,128)(2,1)}, u32[]{:S(2)}, u32[]{:S(2)}) %collective-permute-start.4) | collective-permute-done | bytes 1572896 | tf_op jit(solution)/shard_map/ppermute | solution.py:16
  217.0 2.0 pad_maximum_fusion
  219.0 12.8 %fusion = (f32[4,768]{1,0:T(4,128)S(1)}, f32[4,768,2304]{2,1,0:T(8,128)}) fusion(pred[768,2304]{1,0:T(8,128)(4,1)S(1)} %copy-done.3, bf16[2,2304,4,128]{3,1,2,0:T(8,128)(2,1)S(1)} %pad_maximum_fusion, f32[768,4,128]{2,0,1:T(8,128)S(1)} %copy-done.5, f32[128]{0:T(128)S(1)} %get-tuple-element.10, f32[768,4]{0,1:T(4,128)S(1)} %add_rsqrt_fusion), kind=kOutput, calls=%fused_computation.1 | convolution fusion | flops 1834349568 | bytes 34038272 | tf_op jit(solution)/shard_map/qhd,khd->hqk/dot_general | solution.py:74
  231.9 12.9 %fusion.12 = bf16[768,4,128]{0,2,1:T(8,128)(2,1)S(1)} fusion(f32[768,4]{0,1:T(4,128)S(1)} %bitcast.54, f32[4,768,2304]{2,1,0:T(8,128)} %get-tuple-element.13, pred[768,2304]{1,0:T(8,128)(4,1)S(1)} %copy-done.4, bf16[2,2304,4,128]{3,1,2,0:T(8,128)(2,1)} %copy-done.1), kind=kOutput, calls=%fused_computation.21 | convolution fusion | flops 1833959424 | bytes 33239040 | tf_op jit(solution)/shard_map/hqk,khd->qhd/dot_general | solution.py:79
  (43 shorter events, 6.0 us)
Async XLA Ops:
  2.8 60.3 %copy-start = (bf16[768,3072]{1,0:T(8,128)(2,1)S(1)}, bf16[768,3072]{1,0:T(8,128)(2,1)}, u32[]{:S(2)}) copy-start(bf16[768,3072]{1,0:T(8,128)(2,1)} %param.6) | copy-start | bytes 14155780
  2.9 61.7 %copy-start.7 = (f32[2,3072]{1,0:T(2,128)S(1)}, f32[2,3072]{1,0:T(2,128)}, u32[]{:S(2)}) copy-start(f32[2,3072]{1,0:T(2,128)} %param.7) | copy-start | bytes 73732
  2.9 110.7 %copy-start.8 = (f32[2,128]{1,0:T(2,128)S(1)}, f32[2,128]{1,0:T(2,128)}, u32[]{:S(2)}) copy-start(f32[2,128]{1,0:T(2,128)} %param.10) | copy-start | bytes 3076
  2.9 56.3 %collective-permute-start = (bf16[768,3,512]{0,2,1:T(8,128)(2,1)S(1)}, bf16[768,3,512]{0,2,1:T(8,128)(2,1)S(1)}, u32[]{:S(2)}, u32[]{:S(2)}) collective-permute-start(bf16[768,3,512]{0,2,1:T(8,128)(2,1)S(1)} %copy.31), channel_id=1, source_target_pairs={{0,4},{4,8},{8,12},{12,0},{1,5},{5,9},{9,13},{13,1},{2,6},{6,10},{... | collective-permute-start | bytes 7077896 | tf_op jit(solution)/shard_map/ppermute | solution.py:49
  59.2 5.3 %copy-start.10 = (bf16[768,3,512]{0,2,1:T(8,128)(2,1)}, bf16[768,3,512]{0,2,1:T(8,128)(2,1)S(1)}, u32[]{:S(2)}) copy-start(bf16[768,3,512]{0,2,1:T(8,128)(2,1)S(1)} %collective-permute-done) | copy-start | bytes 7077892
  59.2 54.3 %collective-permute-start.1 = (bf16[768,3,512]{0,2,1:T(8,128)(2,1)S(1)}, bf16[768,3,512]{0,2,1:T(8,128)(2,1)}, u32[]{:S(2)}, u32[]{:S(2)}) collective-permute-start(bf16[768,3,512]{0,2,1:T(8,128)(2,1)S(1)} %collective-permute-done), channel_id=1, source_target_pairs={{0,4},{4,8},{8,12},{12,0},{1,5},{5,9},{9,13},{13,1},{2,6},{6,10},{... | collective-permute-start | bytes 7077896 | tf_op jit(solution)/shard_map/ppermute | solution.py:49
  113.6 53.5 %collective-permute-start.2 = (bf16[768,3,512]{0,2,1:T(8,128)(2,1)}, bf16[768,3,512]{0,2,1:T(8,128)(2,1)S(1)}, u32[]{:S(2)}, u32[]{:S(2)}) collective-permute-start(bf16[768,3,512]{0,2,1:T(8,128)(2,1)} %collective-permute-done.1), channel_id=1, source_target_pairs={{0,4},{4,8},{8,12},{12,0},{1,5},{5,9},{9,13},{13,1},{2,6},{6,10},{... | collective-permute-start | bytes 7077896 | tf_op jit(solution)/shard_map/ppermute | solution.py:49
  113.7 5.2 %copy-start.2 = (bf16[768,3,512]{2,0,1:T(8,128)(2,1)S(1)}, bf16[768,3,512]{2,0,1:T(8,128)(2,1)}, u32[]{:S(2)}) copy-start(bf16[768,3,512]{2,0,1:T(8,128)(2,1)} %param.8) | copy-start | bytes 7077892
  118.8 2.1 copy-start.11
  123.0 44.1 %copy-start.6 = (f32[3,512]{1,0:T(4,128)S(1)}, f32[3,512]{1,0:T(4,128)}, u32[]{:S(2)}) copy-start(f32[3,512]{1,0:T(4,128)} %param.9) | copy-start | bytes 18436
  173.4 13.5 %copy-start.9 = (s32[2,27]{1,0:T(2,128)S(1)}, s32[2,27]{1,0:T(2,128)}, u32[]{:S(2)}) copy-start(s32[2,27]{1,0:T(2,128)} %param.11) | copy-start | bytes 652
  179.8 35.9 %collective-permute-start.4 = (bf16[2,768,4,128]{3,1,2,0:T(8,128)(2,1)}, bf16[2,768,4,128]{3,1,2,0:T(8,128)(2,1)}, u32[]{:S(2)}, u32[]{:S(2)}) collective-permute-start(bf16[2,768,4,128]{3,1,2,0:T(8,128)(2,1)} %pad_maximum_fusion.1), channel_id=1, source_target_pairs={{4,0},{8,4},{12,8},{5,1},{9,5},{13,9},{6,2},{10,6},{14,10},{7,3},{... | collective-permute-start | bytes 4718600 | tf_op jit(solution)/shard_map/ppermute | solution.py:16
  181.1 35.8 %collective-permute-start.3 = (bf16[2,768,4,128]{3,1,2,0:T(8,128)(2,1)}, bf16[2,768,4,128]{3,1,2,0:T(8,128)(2,1)}, u32[]{:S(2)}, u32[]{:S(2)}) collective-permute-start(bf16[2,768,4,128]{3,1,2,0:T(8,128)(2,1)} %pad_maximum_fusion.1), channel_id=1, source_target_pairs={{0,4},{4,8},{8,12},{1,5},{5,9},{9,13},{2,6},{6,10},{10,14},{3,7},{... | collective-permute-start | bytes 4718600 | tf_op jit(solution)/shard_map/ppermute | solution.py:15
  196.0 23.0 %copy-start.3 = (pred[768,2304]{1,0:T(8,128)(4,1)S(1)}, pred[768,2304]{1,0:T(8,128)(4,1)}, u32[]{:S(2)}) copy-start(pred[768,2304]{1,0:T(8,128)(4,1)} %copy.34) | copy-start | bytes 5308420
  196.0 23.0 %copy-start.5 = (f32[768,4,128]{2,0,1:T(8,128)S(1)}, f32[768,4,128]{2,0,1:T(8,128)}, u32[]{:S(2)}) copy-start(f32[768,4,128]{2,0,1:T(8,128)} %copy.35) | copy-start | bytes 4718596
  219.0 12.9 %copy-start.1 = (bf16[2,2304,4,128]{3,1,2,0:T(8,128)(2,1)}, bf16[2,2304,4,128]{3,1,2,0:T(8,128)(2,1)S(1)}, u32[]{:S(2)}) copy-start(bf16[2,2304,4,128]{3,1,2,0:T(8,128)(2,1)S(1)} %pad_maximum_fusion) | copy-start | bytes 14155780
  219.0 12.9 %copy-start.4 = (pred[768,2304]{1,0:T(8,128)(4,1)S(1)}, pred[768,2304]{1,0:T(8,128)(4,1)}, u32[]{:S(2)}) copy-start(pred[768,2304]{1,0:T(8,128)(4,1)} %copy.34) | copy-start | bytes 5308420
